TPU v7x, 32 devices: a whole 2x2x4 slice. The times are simulated.
32 devices in a mesh: group: 1, image: 4 (over z), prow: 4 (over y, x), pcol: 2 (over core).
Axes of the slice: x: 2, y: 2, z: 4, core: 2. Of those that a mesh axis runs over, the one named last changes fastest.
Arguments:
- latent: bfloat16 [4, 32, 64, 640], P(('group', 'image'), 'prow', 'pcol'), may hold values from -6 to 6
- conv_weight: bfloat16 [3, 3, 640, 640], replicated, may hold values from -0.078125 to 0.078125
- w_query: bfloat16 [640, 640], replicated, may hold values from -2 to 2
- w_key: bfloat16 [640, 640], replicated, may hold values from -2 to 2
- w_value: bfloat16 [640, 640], replicated, may hold values from -0.25 to 0.25
- w_out: bfloat16 [640, 640], replicated, may hold values from -0.25 to 0.25
- anchor_index: int32 [4], P('group'), may hold values from 0 to 3, as said below
- block_order: int32 [4, 16], P('group'), may hold values from 0 to 15, each once within a row
- block_count: int32 [4], P('group'), may hold values from 1 to 4, as said below
Outputs:
- features: bfloat16 [4, 32, 64, 640], P(('group', 'image'), 'prow', 'pcol')
- attended: bfloat16 [4, 32, 64, 640], P(('group', 'image'), 'prow', 'pcol')
Inputs may be any that keep to these rules, and one draw needn't show every extreme that they name: `anchor_index`: 4 different images of the batch. `block_count`: some anchor has 4 subject blocks.
All inputs are finite; a program needn't handle non-finite values.
Results may differ from a plain program's by a relative error of at most 0.017.
Values may be sent and summed in bfloat16 or wider, within the bound.
No kernel may reach another device: no remote copies, remote signals or barrier semaphores. Data moves between devices by JAX's collectives and lax.ppermute only.
A program may use at most 128 MiB of HBM per device.

v0:
```python
import jax
import jax.numpy as jnp
from jax import lax
from jax.sharding import PartitionSpec as P

HEAD_DIM = 64
BLOCK = 128
ANCHORS = 4
NSEL = 4


def extended(cells, sides, width):
    for axis, dim in sides:
        count = lax.axis_size(axis)
        ends = count - 1
        head = lax.slice_in_dim(cells, 0, width, axis=dim)
        tail = lax.slice_in_dim(cells, cells.shape[dim] - width, cells.shape[dim], axis=dim)
        cells = jnp.concatenate(
            [
                lax.ppermute(tail, axis, [(i, (i + 1) % count) for i in range(ends)]),
                cells,
                lax.ppermute(head, axis, [((i + 1) % count, i) for i in range(ends)]),
            ],
            axis=dim,
        )
    return cells


def from_root(block, axis, holder):
    block = jnp.where(lax.axis_index(axis) == holder, block, jnp.zeros_like(block))
    return lax.psum(block, axis)


def layer_norm(values):
    centered = values - jnp.mean(values, axis=-1, keepdims=True)
    spread = jnp.mean(centered * centered, axis=-1, keepdims=True)
    return centered * lax.rsqrt(spread + 1e-05)


def grouped_attention(query_cols, every_kv, allowed, group_heads):
    span_cols = group_heads * HEAD_DIM
    value_start = every_kv.shape[1] // 2

    def one_group(group_number):
        offset_col = group_number * span_cols
        group_query = lax.dynamic_slice_in_dim(query_cols, offset_col, span_cols, 1).reshape(
            -1, group_heads, HEAD_DIM
        )
        group_key = lax.dynamic_slice_in_dim(every_kv, offset_col, span_cols, 1).reshape(
            -1, group_heads, HEAD_DIM
        )
        group_value = lax.dynamic_slice_in_dim(
            every_kv, value_start + offset_col, span_cols, 1
        ).reshape(-1, group_heads, HEAD_DIM)
        scores = jnp.einsum(
            "qhd,khd->hqk", group_query, group_key, preferred_element_type=jnp.float32
        ) * HEAD_DIM ** (-0.5)
        scores = jnp.where(allowed[None, None, :], scores, -jnp.inf)
        peak = jnp.max(scores, axis=2, keepdims=True)
        exponent = jnp.exp(scores - peak)
        probs = (exponent / jnp.sum(exponent, axis=2, keepdims=True)).astype(jnp.bfloat16)
        group_out = jnp.einsum(
            "hqk,khd->qhd", probs, group_value, preferred_element_type=jnp.float32
        ).astype(jnp.bfloat16)
        return group_out.reshape(-1, span_cols)

    head_outs = lax.map(one_group, jnp.arange(query_cols.shape[1] // span_cols))
    return head_outs.transpose(1, 0, 2).reshape(-1, query_cols.shape[1])


def shards(
    latent, conv_weight, w_query, w_key, w_value, w_out, anchor_index, block_order, block_count
):
    tile_rows, tile_cols, channels = (latent.shape[1], latent.shape[2], latent.shape[3])
    activated = jax.nn.silu(latent.astype(jnp.float32)).astype(jnp.bfloat16)
    padded = extended(activated, (("prow", 1), ("pcol", 2)), 1)
    running = latent.astype(jnp.float32)
    for row_tap in range(3):
        for col_tap in range(3):
            window = padded[:, row_tap : row_tap + tile_rows, col_tap : col_tap + tile_cols, :]
            running = running + jnp.dot(
                window, conv_weight[row_tap, col_tap], preferred_element_type=jnp.float32
            )
    features = running.astype(jnp.bfloat16)
    tokens = features.reshape(-1, channels)
    normed = layer_norm(tokens.astype(jnp.float32)).astype(jnp.bfloat16)
    queries = jnp.dot(normed, w_query, preferred_element_type=jnp.float32).astype(jnp.bfloat16)
    key_part = jnp.dot(normed, w_key, preferred_element_type=jnp.float32).astype(jnp.bfloat16)
    value_part = jnp.dot(normed, w_value, preferred_element_type=jnp.float32).astype(jnp.bfloat16)
    live_slots = jnp.arange(NSEL)[None, :] < block_count[:, None]
    anchor_live = jnp.repeat(live_slots.reshape(-1), BLOCK)
    keyvals = jnp.concatenate([key_part, value_part], axis=1)
    image_kv = lax.all_gather(keyvals, ("prow", "pcol"), axis=0, tiled=True)
    blocks = image_kv.reshape(-1, BLOCK, 2 * channels)
    patch_count = lax.axis_size("prow") * lax.axis_size("pcol")
    share_rows = NSEL * BLOCK // patch_count
    position = lax.axis_index("prow") * lax.axis_size("pcol") + lax.axis_index("pcol")
    received = []
    for anchor in range(ANCHORS):
        picked = blocks[block_order[anchor, :NSEL]].reshape(NSEL * BLOCK, 2 * channels)
        portion = lax.dynamic_slice_in_dim(picked, position * share_rows, share_rows, 0)
        received.append(from_root(portion, "image", anchor_index[anchor]))
    joined = lax.all_gather(jnp.stack(received, axis=0), ("prow", "pcol"), axis=1, tiled=True)
    anchor_kv = joined.reshape(ANCHORS * NSEL * BLOCK, 2 * channels)
    allowed = jnp.concatenate([jnp.ones((image_kv.shape[0],), jnp.bool_), anchor_live])
    every_kv = jnp.concatenate([image_kv, anchor_kv], axis=0)
    merged = grouped_attention(queries, every_kv, allowed, 2)
    attended = jnp.dot(merged, w_out, preferred_element_type=jnp.float32).astype(jnp.bfloat16)
    return (features, attended.reshape(latent.shape))


def solution(mesh):
    placed = (
        P(("group", "image"), "prow", "pcol", None),
        P(),
        P(),
        P(),
        P(),
        P(),
        P("group"),
        P("group", None),
        P("group"),
    )
    return jax.shard_map(
        shards,
        mesh=mesh,
        in_specs=placed,
        out_specs=(
            P(("group", "image"), "prow", "pcol", None),
            P(("group", "image"), "prow", "pcol", None),
        ),
        check_vma=False,
    )
```

profile of v0, /device:TPU:0, one launch (start us, length us, event | category | flops | bytes accessed | tf_op | source)
XLA Modules:
  0.0 259.8 jit_solution(5241671841525524650)
XLA Ops:
  7.2 1.3 fusion.46
  8.6 5.1 %collective-permute-start = (bf16[1,1,32,640]{3,2,1,0:T(8,128)(2,1)S(1)}, bf16[1,1,32,640]{3,2,1,0:T(8,128)(2,1)S(1)}, u32[]{:S(2)}, u32[]{:S(2)}) collective-permute-start(bf16[1,1,32,640]{3,2,1,0:T(8,128)(2,1)S(1)} %get-tuple-element.108), channel_id=1, source_target_pairs={{0,2},{2,4},{4,6},{1,3},{3,5},{5,7},{8,10},{10,12},{12,14},{9,11},... | collective-permute-start | bytes 122888 | tf_op jit(solution)/shard_map/ppermute | solution.py:20
  13.7 1.3 collective-permute-start.1
  15.0 1.7 convolution_bitcast_fusion.4
  16.8 2.8 %collective-permute-done.1 = bf16[1,1,32,640]{3,2,1,0:T(8,128)(2,1)S(1)} collective-permute-done((bf16[1,1,32,640]{3,2,1,0:T(8,128)(2,1)S(1)}, bf16[1,1,32,640]{3,2,1,0:T(8,128)(2,1)S(1)}, u32[]{:S(2)}, u32[]{:S(2)}) %collective-permute-start.1) | collective-permute-done | bytes 40992 | tf_op jit(solution)/shard_map/ppermute | solution.py:22
  19.7 1.3 collective-permute-start.2
  21.0 1.4 collective-permute-start.3
  22.4 1.6 convolution_bitcast_fusion.1
  27.1 0.7 convert_reduce_fusion
  29.3 0.9 pad_maximum_fusion.1
  33.4 40.0 %all-gather.3.cloned.1.call-done = bf16[2048,1280]{1,0:T(8,128)(2,1)} async-done(((bf16[256,1280]{1,0:T(8,128)(2,1)}), bf16[2048,1280]{1,0:T(8,128)(2,1)}) %all-gather.3.cloned.1.call-update) | async-done | bytes 5242896 | tf_op jit(solution)/shard_map/all_gather | solution.py:93
  73.4 4.3 %gather_fusion.2 = bf16[4,128,1280]{2,1,0:T(8,128)(2,1)} fusion(bf16[16,128,1280]{2,1,0:T(8,128)(2,1)} %bitcast.203, s32[1024]{0:T(1024)S(1)} %get-tuple-element.121), kind=kCustom, calls=%fused_computation.2 | custom fusion | bytes 2621456 | tf_op jit(solution)/shard_map/gather | solution.py:100
  77.6 4.2 %gather_fusion.1 = bf16[4,128,1280]{2,1,0:T(8,128)(2,1)} fusion(bf16[16,128,1280]{2,1,0:T(8,128)(2,1)} %bitcast.204, s32[1024]{0:T(1024)S(1)} %get-tuple-element.122), kind=kCustom, calls=%fused_computation.1 | custom fusion | bytes 2621456 | tf_op jit(solution)/shard_map/gather | solution.py:100
  81.8 4.2 %gather_fusion = bf16[4,128,1280]{2,1,0:T(8,128)(2,1)} fusion(bf16[16,128,1280]{2,1,0:T(8,128)(2,1)} %bitcast.205, s32[1024]{0:T(1024)S(1)} %get-tuple-element.123), kind=kCustom, calls=%fused_computation | custom fusion | bytes 2621456 | tf_op jit(solution)/shard_map/gather | solution.py:100
  86.0 3.1 %gather_fusion.3 = bf16[4,128,1280]{2,1,0:T(8,128)(2,1)S(1)} fusion(bf16[16,128,1280]{2,1,0:T(8,128)(2,1)} %bitcast.206, s32[1024]{0:T(1024)S(1)} %get-tuple-element.120), kind=kCustom, calls=%fused_computation.3 | custom fusion | bytes 2621456 | tf_op jit(solution)/shard_map/gather | solution.py:100
  89.1 1.6 select_bitcast_fusion.1
  90.8 1.6 select_bitcast_fusion.2
  92.4 1.6 select_bitcast_fusion.3
  94.0 0.7 select_bitcast_fusion
  94.8 40.7 %all-reduce.4.cloned.1.call-done = (bf16[1,64,1280]{2,1,0:T(8,128)(2,1)}, bf16[1,64,1280]{2,1,0:T(8,128)(2,1)}, bf16[1,64,1280]{2,1,0:T(8,128)(2,1)}, bf16[1,64,1280]{2,1,0:T(8,128)(2,1)}) async-done(((bf16[1,64,1280]{2,1,0:T(8,128)(2,1)}, bf16[1,64,1280]{2,1,0:T(8,128)(2,1)}, bf16[1,64,1280]{2,1,0:T(8,128)(2,1)}, bf16[1,64,1280]{2,1,0:T(8,128)(2,1)}), (bf16[1,64,1280]{2,1,0:T(8,128)(2,1)}, ...) | async-done | bytes 655376 | tf_op jit(solution)/shard_map/psum | solution.py:31
  135.5 2.1 pad_maximum_fusion.2
  137.8 1.6 convolution_convert_fusion.1
  139.4 39.0 %all-gather.5.cloned.1.call-done = bf16[4,512,1280]{2,1,0:T(8,128)(2,1)} async-done(((bf16[4,64,1280]{2,1,0:T(8,128)(2,1)}), bf16[4,512,1280]{2,1,0:T(8,128)(2,1)}) %all-gather.5.cloned.1.call-update) | async-done | bytes 5242896 | tf_op jit(solution)/shard_map/all_gather | solution.py:103
  178.4 9.9 %pad_maximum_fusion = bf16[4096,1280]{1,0:T(8,128)(2,1)} fusion(bf16[2048,1280]{1,0:T(8,128)(2,1)} %bitcast.207, bf16[2048,1280]{1,0:T(8,128)(2,1)} %all-gather.3.cloned.1.call-done), kind=kLoop, calls=%fused_computation.23 | loop fusion | flops 20971520 | bytes 20971520 | tf_op jit(solution)/shard_map/concatenate | solution.py:106
  188.3 14.3 %copy.11 = bf16[4096,1280]{0,1:T(8,128)(2,1)} copy(bf16[4096,1280]{1,0:T(8,128)(2,1)} %pad_maximum_fusion) | data formatting | bytes 20971520 | tf_op jit(solution)/shard_map/while | solution.py:67
  202.6 48.2 %while.12 = (s32[]{:T(128)}, bf16[5,256,128]{1,2,0:T(8,128)(2,1)}, s32[5]{0:T(128)S(1)}, bf16[4096,1280]{0,1:T(8,128)(2,1)}, pred[4096]{0:T(1024)(128)(4,1)S(1)}...) while((s32[]{:T(128)}, bf16[5,256,128]{1,2,0:T(8,128)(2,1)}, ...), condition=%wide.region_9.10_spmd, body=%wide.region_6.9_spmd.sunk | while | flops 824222208 | bytes 7942902 | solution.py:67
  202.6 0.6 dynamic_slice.53
  203.9 1.7 constant_dynamic-slice_fusion.5
  205.7 3.0 %fusion.91 = f32[2,256]{1,0:T(2,128)S(1)} fusion(pred[4096]{0:T(1024)(128)(4,1)S(1)} %get-tuple-element.193, bf16[256,2,64]{0,2,1:T(8,128)(2,1)S(1)} %bitcast.212, bf16[4096,2,64]{0,2,1:T(8,128)(2,1)S(1)} %bitcast.200), kind=kOutput, calls=%fused_computation.118.clone.1 | convolution fusion | flops 276828160 | bytes 1120256 | tf_op jit(solution)/shard_map/while/body/eval_jaxpr/sub | solution.py:60
  208.7 2.9 %fusion.92 = bf16[2,64,256]{2,1,0:T(8,128)(2,1)S(1)} fusion(bf16[4096,2,64]{0,2,1:T(8,128)(2,1)S(1)} %bitcast.202, f32[2,256]{1,0:T(2,128)S(1)} %fusion.91, pred[4096]{0:T(1024)(128)(4,1)S(1)} %get-tuple-element.193, bf16[256,2,64]{0,2,1:T(8,128)(2,1)S(1)} %bitcast.213, bf16[4096,2,64]{0,2,1:T(8,128)(2,1)S(1)} %bitcast.201), kind=kOutput, calls=%fused_computation.14.clone.1 | convolution fusion | flops 547394048 | bytes 2234368 | tf_op jit(solution)/shard_map/while/body/eval_jaxpr/hqk,khd->qhd/dot_general | solution.py:62
  211.6 0.6 constant_dynamic-update-slice_fusion.2
  213.5 1.7 constant_dynamic-slice_fusion.5
  215.3 3.0 %fusion.91 = f32[2,256]{1,0:T(2,128)S(1)} fusion(pred[4096]{0:T(1024)(128)(4,1)S(1)} %get-tuple-element.193, bf16[256,2,64]{0,2,1:T(8,128)(2,1)S(1)} %bitcast.212, bf16[4096,2,64]{0,2,1:T(8,128)(2,1)S(1)} %bitcast.200), kind=kOutput, calls=%fused_computation.118.clone.1 | convolution fusion | flops 276828160 | bytes 1120256 | tf_op jit(solution)/shard_map/while/body/eval_jaxpr/sub | solution.py:60
  218.3 2.9 %fusion.92 = bf16[2,64,256]{2,1,0:T(8,128)(2,1)S(1)} fusion(bf16[4096,2,64]{0,2,1:T(8,128)(2,1)S(1)} %bitcast.202, f32[2,256]{1,0:T(2,128)S(1)} %fusion.91, pred[4096]{0:T(1024)(128)(4,1)S(1)} %get-tuple-element.193, bf16[256,2,64]{0,2,1:T(8,128)(2,1)S(1)} %bitcast.213, bf16[4096,2,64]{0,2,1:T(8,128)(2,1)S(1)} %bitcast.201), kind=kOutput, calls=%fused_computation.14.clone.1 | convolution fusion | flops 547394048 | bytes 2234368 | tf_op jit(solution)/shard_map/while/body/eval_jaxpr/hqk,khd->qhd/dot_general | solution.py:62
  221.2 0.6 constant_dynamic-update-slice_fusion.2
  223.1 1.7 constant_dynamic-slice_fusion.5
  225.0 3.0 %fusion.91 = f32[2,256]{1,0:T(2,128)S(1)} fusion(pred[4096]{0:T(1024)(128)(4,1)S(1)} %get-tuple-element.193, bf16[256,2,64]{0,2,1:T(8,128)(2,1)S(1)} %bitcast.212, bf16[4096,2,64]{0,2,1:T(8,128)(2,1)S(1)} %bitcast.200), kind=kOutput, calls=%fused_computation.118.clone.1 | convolution fusion | flops 276828160 | bytes 1120256 | tf_op jit(solution)/shard_map/while/body/eval_jaxpr/sub | solution.py:60
  228.0 2.9 %fusion.92 = bf16[2,64,256]{2,1,0:T(8,128)(2,1)S(1)} fusion(bf16[4096,2,64]{0,2,1:T(8,128)(2,1)S(1)} %bitcast.202, f32[2,256]{1,0:T(2,128)S(1)} %fusion.91, pred[4096]{0:T(1024)(128)(4,1)S(1)} %get-tuple-element.193, bf16[256,2,64]{0,2,1:T(8,128)(2,1)S(1)} %bitcast.213, bf16[4096,2,64]{0,2,1:T(8,128)(2,1)S(1)} %bitcast.201), kind=kOutput, calls=%fused_computation.14.clone.1 | convolution fusion | flops 547394048 | bytes 2234368 | tf_op jit(solution)/shard_map/while/body/eval_jaxpr/hqk,khd->qhd/dot_general | solution.py:62
  230.9 0.6 constant_dynamic-update-slice_fusion.2
  232.8 1.7 constant_dynamic-slice_fusion.5
  234.6 3.0 %fusion.91 = f32[2,256]{1,0:T(2,128)S(1)} fusion(pred[4096]{0:T(1024)(128)(4,1)S(1)} %get-tuple-element.193, bf16[256,2,64]{0,2,1:T(8,128)(2,1)S(1)} %bitcast.212, bf16[4096,2,64]{0,2,1:T(8,128)(2,1)S(1)} %bitcast.200), kind=kOutput, calls=%fused_computation.118.clone.1 | convolution fusion | flops 276828160 | bytes 1120256 | tf_op jit(solution)/shard_map/while/body/eval_jaxpr/sub | solution.py:60
  237.6 2.9 %fusion.92 = bf16[2,64,256]{2,1,0:T(8,128)(2,1)S(1)} fusion(bf16[4096,2,64]{0,2,1:T(8,128)(2,1)S(1)} %bitcast.202, f32[2,256]{1,0:T(2,128)S(1)} %fusion.91, pred[4096]{0:T(1024)(128)(4,1)S(1)} %get-tuple-element.193, bf16[256,2,64]{0,2,1:T(8,128)(2,1)S(1)} %bitcast.213, bf16[4096,2,64]{0,2,1:T(8,128)(2,1)S(1)} %bitcast.201), kind=kOutput, calls=%fused_computation.14.clone.1 | convolution fusion | flops 547394048 | bytes 2234368 | tf_op jit(solution)/shard_map/while/body/eval_jaxpr/hqk,khd->qhd/dot_general | solution.py:62
  240.5 0.6 constant_dynamic-update-slice_fusion.2
  242.4 1.7 constant_dynamic-slice_fusion.5
  244.2 3.0 %fusion.91 = f32[2,256]{1,0:T(2,128)S(1)} fusion(pred[4096]{0:T(1024)(128)(4,1)S(1)} %get-tuple-element.193, bf16[256,2,64]{0,2,1:T(8,128)(2,1)S(1)} %bitcast.212, bf16[4096,2,64]{0,2,1:T(8,128)(2,1)S(1)} %bitcast.200), kind=kOutput, calls=%fused_computation.118.clone.1 | convolution fusion | flops 276828160 | bytes 1120256 | tf_op jit(solution)/shard_map/while/body/eval_jaxpr/sub | solution.py:60
  247.3 2.9 %fusion.92 = bf16[2,64,256]{2,1,0:T(8,128)(2,1)S(1)} fusion(bf16[4096,2,64]{0,2,1:T(8,128)(2,1)S(1)} %bitcast.202, f32[2,256]{1,0:T(2,128)S(1)} %fusion.91, pred[4096]{0:T(1024)(128)(4,1)S(1)} %get-tuple-element.193, bf16[256,2,64]{0,2,1:T(8,128)(2,1)S(1)} %bitcast.213, bf16[4096,2,64]{0,2,1:T(8,128)(2,1)S(1)} %bitcast.201), kind=kOutput, calls=%fused_computation.14.clone.1 | convolution fusion | flops 547394048 | bytes 2234368 | tf_op jit(solution)/shard_map/while/body/eval_jaxpr/hqk,khd->qhd/dot_general | solution.py:62
  250.2 0.6 constant_dynamic-update-slice_fusion.2
  250.8 2.5 convolution_convert_fusion
  (66 shorter events, 8.6 us)
Async XLA Ops:
  7.2 21.2 %copy-start = (bf16[640,640]{1,0:T(8,128)(2,1)S(1)}, bf16[640,640]{1,0:T(8,128)(2,1)}, u32[]{:S(2)}) copy-start(bf16[640,640]{1,0:T(8,128)(2,1)} %param.15) | copy-start | bytes 2457604
  7.2 66.2 %all-gather.3.cloned.1.call-start = ((), (), s32[]{:S(2)}) async-start(), calls=%async_computation | async-start | bytes 5898240 | tf_op jit(solution)/shard_map/all_gather | solution.py:93
  7.2 16.8 %copy-start.3 = (bf16[3,3,640,640]{3,2,1,0:T(8,128)(2,1)S(1)}, bf16[3,3,640,640]{3,2,1,0:T(8,128)(2,1)}, u32[]{:S(2)}) copy-start(bf16[3,3,640,640]{3,2,1,0:T(8,128)(2,1)} %param.12) | copy-start | bytes 22118404
  8.6 8.2 %collective-permute-start = (bf16[1,1,32,640]{3,2,1,0:T(8,128)(2,1)S(1)}, bf16[1,1,32,640]{3,2,1,0:T(8,128)(2,1)S(1)}, u32[]{:S(2)}, u32[]{:S(2)}) collective-permute-start(bf16[1,1,32,640]{3,2,1,0:T(8,128)(2,1)S(1)} %get-tuple-element.108), channel_id=1, source_target_pairs={{0,2},{2,4},{4,6},{1,3},{3,5},{5,7},{8,10},{10,12},{12,14},{9,11},... | collective-permute-start | bytes 122888 | tf_op jit(solution)/shard_map/ppermute | solution.py:20
  13.7 5.9 %collective-permute-start.1 = (bf16[1,1,32,640]{3,2,1,0:T(8,128)(2,1)S(1)}, bf16[1,1,32,640]{3,2,1,0:T(8,128)(2,1)S(1)}, u32[]{:S(2)}, u32[]{:S(2)}) collective-permute-start(bf16[1,1,32,640]{3,2,1,0:T(8,128)(2,1)S(1)} %get-tuple-element.109), channel_id=1, source_target_pairs={{2,0},{4,2},{6,4},{3,1},{5,3},{7,5},{10,8},{12,10},{14,12},{11,9},... | collective-permute-start | bytes 122888 | tf_op jit(solution)/shard_map/ppermute | solution.py:22
  19.7 4.8 %collective-permute-start.2 = (bf16[1,10,1,640]{3,2,1,0:T(2,128)(2,1)S(1)}, bf16[1,10,1,640]{3,2,1,0:T(2,128)(2,1)S(1)}, u32[]{:S(2)}, u32[]{:S(2)}) collective-permute-start(bf16[1,10,1,640]{3,2,1,0:T(2,128)(2,1)S(1)} %get-tuple-element.106), channel_id=1, source_target_pairs={{0,1},{2,3},{4,5},{6,7},{8,9},{10,11},{12,13},{14,15},{16,17},{18,... | collective-permute-start | bytes 38408 | tf_op jit(solution)/shard_map/ppermute | solution.py:20
  21.0 6.1 %copy-start.2 = (bf16[1,8,32,640]{3,2,1,0:T(8,128)(2,1)S(1)}, bf16[1,8,32,640]{3,2,1,0:T(8,128)(2,1)}, u32[]{:S(2)}) copy-start(bf16[1,8,32,640]{3,2,1,0:T(8,128)(2,1)} %param.11) | copy-start | bytes 983044
  21.0 3.5 %collective-permute-start.3 = (bf16[1,10,1,640]{3,2,1,0:T(2,128)(2,1)S(1)}, bf16[1,10,1,640]{3,2,1,0:T(2,128)(2,1)S(1)}, u32[]{:S(2)}, u32[]{:S(2)}) collective-permute-start(bf16[1,10,1,640]{3,2,1,0:T(2,128)(2,1)S(1)} %get-tuple-element.107), channel_id=1, source_target_pairs={{1,0},{3,2},{5,4},{7,6},{9,8},{11,10},{13,12},{15,14},{17,16},{19,... | collective-permute-start | bytes 38408 | tf_op jit(solution)/shard_map/ppermute | solution.py:22
  25.6 3.2 %copy-start.4 = (bf16[640,640]{1,0:T(8,128)(2,1)S(1)}, bf16[640,640]{1,0:T(8,128)(2,1)}, u32[]{:S(2)}) copy-start(bf16[640,640]{1,0:T(8,128)(2,1)} %param.14) | copy-start | bytes 2457604
  26.6 3.7 %copy-start.5 = (s32[4]{0:T(128)S(1)}, s32[4]{0:T(128)}, u32[]{:S(2)}) copy-start(s32[4]{0:T(128)} %param.17) | copy-start | bytes 52
  26.6 6.7 %copy-start.6 = (s32[4,16]{1,0:T(4,128)S(1)}, s32[4,16]{1,0:T(4,128)}, u32[]{:S(2)}) copy-start(s32[4,16]{1,0:T(4,128)} %param.18) | copy-start | bytes 772
  27.8 61.4 %copy-start.1 = (bf16[1,8,32,640]{3,2,1,0:T(8,128)(2,1)}, bf16[1,8,32,640]{3,2,1,0:T(8,128)(2,1)S(1)}, u32[]{:S(2)}) copy-start(bf16[1,8,32,640]{3,2,1,0:T(8,128)(2,1)S(1)} %get-tuple-element.119) | copy-start | bytes 983044
  30.2 107.3 %copy-start.7 = (s32[4]{0:T(128)S(1)}, s32[4]{0:T(128)}, u32[]{:S(2)}) copy-start(s32[4]{0:T(128)} %param.19) | copy-start | bytes 52
  30.3 105.2 %all-reduce.4.cloned.1.call-start = ((), (), s32[]{:S(2)}) async-start(), calls=%async_computation.2 | async-start | bytes 1310720 | tf_op jit(solution)/shard_map/psum | solution.py:31
  94.7 83.7 %all-gather.5.cloned.1.call-start = ((), (), s32[]{:S(2)}) async-start(), calls=%async_computation.1 | async-start | bytes 5898240 | tf_op jit(solution)/shard_map/all_gather | solution.py:103
Sparse Core Ops, SparseCore 0:
  30.4 42.9 all-gather.2
  94.8 40.5 all-reduce.3
  137.7 40.7 all-gather.4
where the time goes:
time: 261 us; the launch traced here: 260 us
  waiting for transfers between devices  123 us (47%)
  local copies, waits for them, and re-layouts  46.3 us (18%)
  matrix products  41.2 us (16%)
  other arithmetic  20.5 us (8%)
  between operations  16.5 us (6%)
  starting transfers between devices  9.26 us (4%)
  loops' own time  3.44 us (1%)
    psum x1, waiting for transfers between devices, from_root(): return lax.psum(block, axis)  40.7 us
    all_gather x1, waiting for transfers between devices, shards(): image_kv = lax.all_gather(keyvals, ('prow', 'pcol'), axis=0, tiled=True)  40 us
    all_gather x1, waiting for transfers between devices, shards(): lax.all_gather(jnp.stack(received, axis=0), ('prow', 'pcol'), axis=1, til...  39 us
    gather x4, local copies, waits for them, and re-layouts, shards(): blocks[block_order[anchor, :NSEL]].reshape(NSEL * BLOCK, 2 * channels)  15.8 us
    sub x5, matrix products, one_group(): exponent = jnp.exp(scores - peak)  15.1 us
    dot_general x5, matrix products, one_group(): jnp.einsum('hqk,khd->qhd', probs, group_value, preferred_element_type=jnp...  14.4 us
    while x1, local copies, waits for them, and re-layouts, grouped_attention(): head_outs = lax.map(one_group, jnp.arange(query_cols.shape[1] // span_cols))  14.3 us
    concatenate x1, other arithmetic, shards(): every_kv = jnp.concatenate([image_kv, anchor_kv], axis=0)  9.91 us
  transfers between devices with their start and end apart: 7, of which 4 were waited for; matrix products, arithmetic and copies ran while one was open for 2% of the time, Pallas kernels for 0%

commit v1 on v0

--- a/solution.py
+++ b/solution.py
@@ -28,7 +28,7 @@
 
 def from_root(block, axis, holder):
     block = jnp.where(lax.axis_index(axis) == holder, block, jnp.zeros_like(block))
-    return lax.psum(block, axis)
+    return jnp.sum(lax.all_gather(block, axis), axis=0)
 
 
 def layer_norm(values):

time: 261 us -> 280 us (1.073)
  blocking collectives: 0 us -> 66.5 us
  waiting for transfers between devices: 123 us -> 81.5 us
  other arithmetic: 20.5 us -> 15.2 us
    all_gather x0 -> x4, blocking collectives: none -> 66.5 us  [from_root(): return jnp.sum(lax.all_gather(block, axis), axis=0)]
    psum x1 -> x0, waiting for transfers between devices: 40.7 us -> none  [from_root(): return lax.psum(block, axis)]
    another operation x5 -> x1, other arithmetic: 7.6 us -> 0.94 us  [shards(): jnp.stack(received, axis=0)]
  transfers between devices with their start and end apart: 7 -> 6, of which waited for: 4 -> 3; matrix products, arithmetic and copies ran while one was open for 2% -> 2% of each run, Pallas kernels for 0% -> 0%
where the time goes in v1:
time: 280 us; the launch traced here: 278 us
  waiting for transfers between devices  81.5 us (29%)
  blocking collectives  66.5 us (24%)
  local copies, waits for them, and re-layouts  44.2 us (16%)
  matrix products  41.2 us (15%)
  between operations  17 us (6%)
  other arithmetic  15.2 us (5%)
  starting transfers between devices  9.22 us (3%)
  loops' own time  3.64 us (1%)
    all_gather x4, blocking collectives, from_root(): return jnp.sum(lax.all_gather(block, axis), axis=0)  66.5 us
    all_gather x1, waiting for transfers between devices, shards(): image_kv = lax.all_gather(keyvals, ('prow', 'pcol'), axis=0, tiled=True)  39.8 us
    all_gather x1, waiting for transfers between devices, shards(): lax.all_gather(jnp.stack(received, axis=0), ('prow', 'pcol'), axis=1, til...  38.8 us
    sub x5, matrix products, one_group(): exponent = jnp.exp(scores - peak)  15.1 us
    dot_general x5, matrix products, one_group(): jnp.einsum('hqk,khd->qhd', probs, group_value, preferred_element_type=jnp...  14.4 us
    while x1, local copies, waits for them, and re-layouts, grouped_attention(): head_outs = lax.map(one_group, jnp.arange(query_cols.shape[1] // span_cols))  14.3 us
    gather x4, local copies, waits for them, and re-layouts, shards(): blocks[block_order[anchor, :NSEL]].reshape(NSEL * BLOCK, 2 * channels)  13.6 us
    concatenate x1, other arithmetic, shards(): every_kv = jnp.concatenate([image_kv, anchor_kv], axis=0)  9.74 us
  transfers between devices with their start and end apart: 6, of which 3 were waited for; matrix products, arithmetic and copies ran while one was open for 2% of the time, Pallas kernels for 0%

profile of v1, /device:TPU:0, one launch (start us, length us, event | category | flops | bytes accessed | tf_op | source)
XLA Modules:
  0.0 278.5 jit_solution(10333131218956942485)
XLA Ops:
  7.2 1.3 fusion.46
  8.6 5.1 %collective-permute-start = (bf16[1,1,32,640]{3,2,1,0:T(8,128)(2,1)S(1)}, bf16[1,1,32,640]{3,2,1,0:T(8,128)(2,1)S(1)}, u32[]{:S(2)}, u32[]{:S(2)}) collective-permute-start(bf16[1,1,32,640]{3,2,1,0:T(8,128)(2,1)S(1)} %get-tuple-element.104), channel_id=1, source_target_pairs={{0,2},{2,4},{4,6},{1,3},{3,5},{5,7},{8,10},{10,12},{12,14},{9,11},... | collective-permute-start | bytes 122888 | tf_op jit(solution)/shard_map/ppermute | solution.py:20
  13.7 1.3 collective-permute-start.1
  15.0 1.7 convolution_bitcast_fusion.4
  16.8 2.8 %collective-permute-done.1 = bf16[1,1,32,640]{3,2,1,0:T(8,128)(2,1)S(1)} collective-permute-done((bf16[1,1,32,640]{3,2,1,0:T(8,128)(2,1)S(1)}, bf16[1,1,32,640]{3,2,1,0:T(8,128)(2,1)S(1)}, u32[]{:S(2)}, u32[]{:S(2)}) %collective-permute-start.1) | collective-permute-done | bytes 40992 | tf_op jit(solution)/shard_map/ppermute | solution.py:22
  19.7 1.3 collective-permute-start.2
  21.0 1.4 collective-permute-start.3
  22.4 1.6 convolution_bitcast_fusion.1
  27.1 0.7 convert_reduce_fusion
  29.3 0.9 pad_maximum_fusion.1
  30.3 0.7 fusion.65
  33.6 39.8 %all-gather.7.cloned.1.call-done = bf16[2048,1280]{1,0:T(8,128)(2,1)} async-done(((bf16[256,1280]{1,0:T(8,128)(2,1)}), bf16[2048,1280]{1,0:T(8,128)(2,1)}) %all-gather.7.cloned.1.call-update) | async-done | bytes 5242896 | tf_op jit(solution)/shard_map/all_gather | solution.py:93
  73.3 3.1 %gather_fusion = bf16[4,128,1280]{2,1,0:T(8,128)(2,1)S(1)} fusion(bf16[16,128,1280]{2,1,0:T(8,128)(2,1)} %bitcast.203, s32[1024]{0:T(1024)S(1)} %get-tuple-element.119), kind=kCustom, calls=%fused_computation | custom fusion | bytes 2621456 | tf_op jit(solution)/shard_map/gather | solution.py:100
  76.5 18.1 %all-gather = bf16[256,1280]{1,0:T(8,128)(2,1)S(1)} all-gather(bf16[64,1280]{1,0:T(8,128)(2,1)S(1)} %dynamic-slice_select_fusion.3), channel_id=2, replica_groups=mesh['group'=1,'image'=4,'prow'=4,'pcol'=2] {'image'}, dimensions={0}, use_global_device_ids=true | all-gather | bytes 819200 | tf_op jit(solution)/shard_map/all_gather | solution.py:31
  94.6 4.2 %gather_fusion.1 = bf16[4,128,1280]{2,1,0:T(8,128)(2,1)} fusion(bf16[16,128,1280]{2,1,0:T(8,128)(2,1)} %bitcast.204, s32[1024]{0:T(1024)S(1)} %get-tuple-element.118), kind=kCustom, calls=%fused_computation.1 | custom fusion | bytes 2621456 | tf_op jit(solution)/shard_map/gather | solution.py:100
  98.9 1.0 dynamic-slice_select_fusion.2
  99.8 16.3 %all-gather.1 = bf16[256,1280]{1,0:T(8,128)(2,1)S(1)} all-gather(bf16[64,1280]{1,0:T(8,128)(2,1)S(1)} %dynamic-slice_select_fusion.2), channel_id=3, replica_groups=mesh['group'=1,'image'=4,'prow'=4,'pcol'=2] {'image'}, dimensions={0}, use_global_device_ids=true | all-gather | bytes 819200 | tf_op jit(solution)/shard_map/all_gather | solution.py:31
  116.3 3.1 %gather_fusion.2 = bf16[4,128,1280]{2,1,0:T(8,128)(2,1)S(1)} fusion(bf16[16,128,1280]{2,1,0:T(8,128)(2,1)} %bitcast.205, s32[1024]{0:T(1024)S(1)} %get-tuple-element.117), kind=kCustom, calls=%fused_computation.2 | custom fusion | bytes 2621456 | tf_op jit(solution)/shard_map/gather | solution.py:100
  119.5 16.7 %all-gather.2 = bf16[256,1280]{1,0:T(8,128)(2,1)S(1)} all-gather(bf16[64,1280]{1,0:T(8,128)(2,1)S(1)} %dynamic-slice_select_fusion.1), channel_id=4, replica_groups=mesh['group'=1,'image'=4,'prow'=4,'pcol'=2] {'image'}, dimensions={0}, use_global_device_ids=true | all-gather | bytes 819200 | tf_op jit(solution)/shard_map/all_gather | solution.py:31
  136.3 3.1 %gather_fusion.3 = bf16[4,128,1280]{2,1,0:T(8,128)(2,1)S(1)} fusion(bf16[16,128,1280]{2,1,0:T(8,128)(2,1)} %bitcast.206, s32[1024]{0:T(1024)S(1)} %get-tuple-element.116), kind=kCustom, calls=%fused_computation.3 | custom fusion | bytes 2621456 | tf_op jit(solution)/shard_map/gather | solution.py:100
  139.5 15.4 %all-gather.3 = bf16[256,1280]{1,0:T(8,128)(2,1)S(1)} all-gather(bf16[64,1280]{1,0:T(8,128)(2,1)S(1)} %dynamic-slice_select_fusion), channel_id=5, replica_groups=mesh['group'=1,'image'=4,'prow'=4,'pcol'=2] {'image'}, dimensions={0}, use_global_device_ids=true | all-gather | bytes 819200 | tf_op jit(solution)/shard_map/all_gather | solution.py:31
  155.0 0.9 pad_maximum_fusion.2
  156.2 1.6 convolution_convert_fusion.1
  157.8 38.8 %all-gather.9.cloned.1.call-done = bf16[4,512,1280]{2,1,0:T(8,128)(2,1)} async-done(((bf16[4,64,1280]{2,1,0:T(8,128)(2,1)}), bf16[4,512,1280]{2,1,0:T(8,128)(2,1)}) %all-gather.9.cloned.1.call-update) | async-done | bytes 5242896 | tf_op jit(solution)/shard_map/all_gather | solution.py:103
  196.7 9.7 %pad_maximum_fusion = bf16[4096,1280]{1,0:T(8,128)(2,1)} fusion(bf16[2048,1280]{1,0:T(8,128)(2,1)} %bitcast.207, bf16[2048,1280]{1,0:T(8,128)(2,1)} %all-gather.7.cloned.1.call-done), kind=kLoop, calls=%fused_computation.23 | loop fusion | flops 20971520 | bytes 20971520 | tf_op jit(solution)/shard_map/concatenate | solution.py:106
  206.4 14.3 %copy.11 = bf16[4096,1280]{0,1:T(8,128)(2,1)} copy(bf16[4096,1280]{1,0:T(8,128)(2,1)} %pad_maximum_fusion) | data formatting | bytes 20971520 | tf_op jit(solution)/shard_map/while | solution.py:67
  220.7 48.5 %while.12 = (s32[]{:T(128)}, bf16[5,256,128]{1,2,0:T(8,128)(2,1)}, s32[5]{0:T(128)S(1)}, bf16[4096,1280]{0,1:T(8,128)(2,1)}, pred[4096]{0:T(1024)(128)(4,1)S(1)}...) while((s32[]{:T(128)}, bf16[5,256,128]{1,2,0:T(8,128)(2,1)}, ...), condition=%wide.region_9.10_spmd, body=%wide.region_6.9_spmd.sunk | while | flops 824222208 | bytes 7942902 | solution.py:67
  220.7 0.6 dynamic_slice.53
  222.0 1.7 constant_dynamic-slice_fusion.5
  223.9 3.0 %fusion.91 = f32[2,256]{1,0:T(2,128)S(1)} fusion(pred[4096]{0:T(1024)(128)(4,1)S(1)} %get-tuple-element.189, bf16[256,2,64]{0,2,1:T(8,128)(2,1)S(1)} %bitcast.216, bf16[4096,2,64]{0,2,1:T(8,128)(2,1)S(1)} %bitcast.200), kind=kOutput, calls=%fused_computation.118.clone.1 | convolution fusion | flops 276828160 | bytes 1120256 | tf_op jit(solution)/shard_map/while/body/eval_jaxpr/sub | solution.py:60
  226.9 2.9 %fusion.92 = bf16[2,64,256]{2,1,0:T(8,128)(2,1)S(1)} fusion(bf16[4096,2,64]{0,2,1:T(8,128)(2,1)S(1)} %bitcast.202, f32[2,256]{1,0:T(2,128)S(1)} %fusion.91, pred[4096]{0:T(1024)(128)(4,1)S(1)} %get-tuple-element.189, bf16[256,2,64]{0,2,1:T(8,128)(2,1)S(1)} %bitcast.217, bf16[4096,2,64]{0,2,1:T(8,128)(2,1)S(1)} %bitcast.201), kind=kOutput, calls=%fused_computation.14.clone.1 | convolution fusion | flops 547394048 | bytes 2234368 | tf_op jit(solution)/shard_map/while/body/eval_jaxpr/hqk,khd->qhd/dot_general | solution.py:62
  230.4 0.6 dynamic_slice.53
  231.7 1.7 constant_dynamic-slice_fusion.5
  233.6 3.0 %fusion.91 = f32[2,256]{1,0:T(2,128)S(1)} fusion(pred[4096]{0:T(1024)(128)(4,1)S(1)} %get-tuple-element.189, bf16[256,2,64]{0,2,1:T(8,128)(2,1)S(1)} %bitcast.216, bf16[4096,2,64]{0,2,1:T(8,128)(2,1)S(1)} %bitcast.200), kind=kOutput, calls=%fused_computation.118.clone.1 | convolution fusion | flops 276828160 | bytes 1120256 | tf_op jit(solution)/shard_map/while/body/eval_jaxpr/sub | solution.py:60
  236.6 2.9 %fusion.92 = bf16[2,64,256]{2,1,0:T(8,128)(2,1)S(1)} fusion(bf16[4096,2,64]{0,2,1:T(8,128)(2,1)S(1)} %bitcast.202, f32[2,256]{1,0:T(2,128)S(1)} %fusion.91, pred[4096]{0:T(1024)(128)(4,1)S(1)} %get-tuple-element.189, bf16[256,2,64]{0,2,1:T(8,128)(2,1)S(1)} %bitcast.217, bf16[4096,2,64]{0,2,1:T(8,128)(2,1)S(1)} %bitcast.201), kind=kOutput, calls=%fused_computation.14.clone.1 | convolution fusion | flops 547394048 | bytes 2234368 | tf_op jit(solution)/shard_map/while/body/eval_jaxpr/hqk,khd->qhd/dot_general | solution.py:62
  240.1 0.6 dynamic_slice.53
  241.4 1.7 constant_dynamic-slice_fusion.5
  243.3 3.0 %fusion.91 = f32[2,256]{1,0:T(2,128)S(1)} fusion(pred[4096]{0:T(1024)(128)(4,1)S(1)} %get-tuple-element.189, bf16[256,2,64]{0,2,1:T(8,128)(2,1)S(1)} %bitcast.216, bf16[4096,2,64]{0,2,1:T(8,128)(2,1)S(1)} %bitcast.200), kind=kOutput, calls=%fused_computation.118.clone.1 | convolution fusion | flops 276828160 | bytes 1120256 | tf_op jit(solution)/shard_map/while/body/eval_jaxpr/sub | solution.py:60
  246.3 2.9 %fusion.92 = bf16[2,64,256]{2,1,0:T(8,128)(2,1)S(1)} fusion(bf16[4096,2,64]{0,2,1:T(8,128)(2,1)S(1)} %bitcast.202, f32[2,256]{1,0:T(2,128)S(1)} %fusion.91, pred[4096]{0:T(1024)(128)(4,1)S(1)} %get-tuple-element.189, bf16[256,2,64]{0,2,1:T(8,128)(2,1)S(1)} %bitcast.217, bf16[4096,2,64]{0,2,1:T(8,128)(2,1)S(1)} %bitcast.201), kind=kOutput, calls=%fused_computation.14.clone.1 | convolution fusion | flops 547394048 | bytes 2234368 | tf_op jit(solution)/shard_map/while/body/eval_jaxpr/hqk,khd->qhd/dot_general | solution.py:62
  249.8 0.6 dynamic_slice.53
  251.1 1.7 constant_dynamic-slice_fusion.5
  253.0 3.0 %fusion.91 = f32[2,256]{1,0:T(2,128)S(1)} fusion(pred[4096]{0:T(1024)(128)(4,1)S(1)} %get-tuple-element.189, bf16[256,2,64]{0,2,1:T(8,128)(2,1)S(1)} %bitcast.216, bf16[4096,2,64]{0,2,1:T(8,128)(2,1)S(1)} %bitcast.200), kind=kOutput, calls=%fused_computation.118.clone.1 | convolution fusion | flops 276828160 | bytes 1120256 | tf_op jit(solution)/shard_map/while/body/eval_jaxpr/sub | solution.py:60
  256.0 2.9 %fusion.92 = bf16[2,64,256]{2,1,0:T(8,128)(2,1)S(1)} fusion(bf16[4096,2,64]{0,2,1:T(8,128)(2,1)S(1)} %bitcast.202, f32[2,256]{1,0:T(2,128)S(1)} %fusion.91, pred[4096]{0:T(1024)(128)(4,1)S(1)} %get-tuple-element.189, bf16[256,2,64]{0,2,1:T(8,128)(2,1)S(1)} %bitcast.217, bf16[4096,2,64]{0,2,1:T(8,128)(2,1)S(1)} %bitcast.201), kind=kOutput, calls=%fused_computation.14.clone.1 | convolution fusion | flops 547394048 | bytes 2234368 | tf_op jit(solution)/shard_map/while/body/eval_jaxpr/hqk,khd->qhd/dot_general | solution.py:62
  259.5 0.6 dynamic_slice.53
  260.8 1.7 constant_dynamic-slice_fusion.5
  262.7 3.0 %fusion.91 = f32[2,256]{1,0:T(2,128)S(1)} fusion(pred[4096]{0:T(1024)(128)(4,1)S(1)} %get-tuple-element.189, bf16[256,2,64]{0,2,1:T(8,128)(2,1)S(1)} %bitcast.216, bf16[4096,2,64]{0,2,1:T(8,128)(2,1)S(1)} %bitcast.200), kind=kOutput, calls=%fused_computation.118.clone.1 | convolution fusion | flops 276828160 | bytes 1120256 | tf_op jit(solution)/shard_map/while/body/eval_jaxpr/sub | solution.py:60
  265.7 2.9 %fusion.92 = bf16[2,64,256]{2,1,0:T(8,128)(2,1)S(1)} fusion(bf16[4096,2,64]{0,2,1:T(8,128)(2,1)S(1)} %bitcast.202, f32[2,256]{1,0:T(2,128)S(1)} %fusion.91, pred[4096]{0:T(1024)(128)(4,1)S(1)} %get-tuple-element.189, bf16[256,2,64]{0,2,1:T(8,128)(2,1)S(1)} %bitcast.217, bf16[4096,2,64]{0,2,1:T(8,128)(2,1)S(1)} %bitcast.201), kind=kOutput, calls=%fused_computation.14.clone.1 | convolution fusion | flops 547394048 | bytes 2234368 | tf_op jit(solution)/shard_map/while/body/eval_jaxpr/hqk,khd->qhd/dot_general | solution.py:62
  269.2 2.5 convolution_convert_fusion
  (71 shorter events, 9.2 us)
Async XLA Ops:
  7.2 21.2 %copy-start = (bf16[640,640]{1,0:T(8,128)(2,1)S(1)}, bf16[640,640]{1,0:T(8,128)(2,1)}, u32[]{:S(2)}) copy-start(bf16[640,640]{1,0:T(8,128)(2,1)} %param.15) | copy-start | bytes 2457604
  7.2 66.2 %all-gather.7.cloned.1.call-start = ((), (), s32[]{:S(2)}) async-start(), calls=%async_computation | async-start | bytes 5898240 | tf_op jit(solution)/shard_map/all_gather | solution.py:93
  7.2 16.8 %copy-start.3 = (bf16[3,3,640,640]{3,2,1,0:T(8,128)(2,1)S(1)}, bf16[3,3,640,640]{3,2,1,0:T(8,128)(2,1)}, u32[]{:S(2)}) copy-start(bf16[3,3,640,640]{3,2,1,0:T(8,128)(2,1)} %param.12) | copy-start | bytes 22118404
  8.6 8.2 %collective-permute-start = (bf16[1,1,32,640]{3,2,1,0:T(8,128)(2,1)S(1)}, bf16[1,1,32,640]{3,2,1,0:T(8,128)(2,1)S(1)}, u32[]{:S(2)}, u32[]{:S(2)}) collective-permute-start(bf16[1,1,32,640]{3,2,1,0:T(8,128)(2,1)S(1)} %get-tuple-element.104), channel_id=1, source_target_pairs={{0,2},{2,4},{4,6},{1,3},{3,5},{5,7},{8,10},{10,12},{12,14},{9,11},... | collective-permute-start | bytes 122888 | tf_op jit(solution)/shard_map/ppermute | solution.py:20
  13.7 5.9 %collective-permute-start.1 = (bf16[1,1,32,640]{3,2,1,0:T(8,128)(2,1)S(1)}, bf16[1,1,32,640]{3,2,1,0:T(8,128)(2,1)S(1)}, u32[]{:S(2)}, u32[]{:S(2)}) collective-permute-start(bf16[1,1,32,640]{3,2,1,0:T(8,128)(2,1)S(1)} %get-tuple-element.105), channel_id=1, source_target_pairs={{2,0},{4,2},{6,4},{3,1},{5,3},{7,5},{10,8},{12,10},{14,12},{11,9},... | collective-permute-start | bytes 122888 | tf_op jit(solution)/shard_map/ppermute | solution.py:22
  19.7 4.8 %collective-permute-start.2 = (bf16[1,10,1,640]{3,2,1,0:T(2,128)(2,1)S(1)}, bf16[1,10,1,640]{3,2,1,0:T(2,128)(2,1)S(1)}, u32[]{:S(2)}, u32[]{:S(2)}) collective-permute-start(bf16[1,10,1,640]{3,2,1,0:T(2,128)(2,1)S(1)} %get-tuple-element.102), channel_id=1, source_target_pairs={{0,1},{2,3},{4,5},{6,7},{8,9},{10,11},{12,13},{14,15},{16,17},{18,... | collective-permute-start | bytes 38408 | tf_op jit(solution)/shard_map/ppermute | solution.py:20
  21.0 6.1 %copy-start.2 = (bf16[1,8,32,640]{3,2,1,0:T(8,128)(2,1)S(1)}, bf16[1,8,32,640]{3,2,1,0:T(8,128)(2,1)}, u32[]{:S(2)}) copy-start(bf16[1,8,32,640]{3,2,1,0:T(8,128)(2,1)} %param.11) | copy-start | bytes 983044
  21.0 3.5 %collective-permute-start.3 = (bf16[1,10,1,640]{3,2,1,0:T(2,128)(2,1)S(1)}, bf16[1,10,1,640]{3,2,1,0:T(2,128)(2,1)S(1)}, u32[]{:S(2)}, u32[]{:S(2)}) collective-permute-start(bf16[1,10,1,640]{3,2,1,0:T(2,128)(2,1)S(1)} %get-tuple-element.103), channel_id=1, source_target_pairs={{1,0},{3,2},{5,4},{7,6},{9,8},{11,10},{13,12},{15,14},{17,16},{19,... | collective-permute-start | bytes 38408 | tf_op jit(solution)/shard_map/ppermute | solution.py:22
  25.6 3.2 %copy-start.4 = (bf16[640,640]{1,0:T(8,128)(2,1)S(1)}, bf16[640,640]{1,0:T(8,128)(2,1)}, u32[]{:S(2)}) copy-start(bf16[640,640]{1,0:T(8,128)(2,1)} %param.14) | copy-start | bytes 2457604
  26.6 3.7 %copy-start.5 = (s32[4]{0:T(128)S(1)}, s32[4]{0:T(128)}, u32[]{:S(2)}) copy-start(s32[4]{0:T(128)} %param.17) | copy-start | bytes 52
  26.6 6.9 %copy-start.6 = (s32[4,16]{1,0:T(4,128)S(1)}, s32[4,16]{1,0:T(4,128)}, u32[]{:S(2)}) copy-start(s32[4,16]{1,0:T(4,128)} %param.18) | copy-start | bytes 772
  27.8 88.5 %copy-start.1 = (bf16[1,8,32,640]{3,2,1,0:T(8,128)(2,1)}, bf16[1,8,32,640]{3,2,1,0:T(8,128)(2,1)S(1)}, u32[]{:S(2)}) copy-start(bf16[1,8,32,640]{3,2,1,0:T(8,128)(2,1)S(1)} %get-tuple-element.115) | copy-start | bytes 983044
  30.2 166.4 %all-gather.9.cloned.1.call-start = ((), (), s32[]{:S(2)}) async-start(), calls=%async_computation.1 | async-start | bytes 5898240 | tf_op jit(solution)/shard_map/all_gather | solution.py:103
  98.8 57.1 %copy-start.7 = (s32[4]{0:T(128)S(1)}, s32[4]{0:T(128)}, u32[]{:S(2)}) copy-start(s32[4]{0:T(128)} %param.19) | copy-start | bytes 52
Sparse Core Ops, SparseCore 0:
  30.4 42.9 all-gather.6
  156.1 40.5 all-gather.8
